TPU v7x, 32 devices: a whole 2x2x4 slice. The times are simulated.
32 devices in a mesh: rep: 4 (over z), fsdp: 8 (over y, x, core).
Axes of the slice: x: 2, y: 2, z: 4, core: 2. Of those that a mesh axis runs over, the one named last changes fastest.
Arguments:
- activations: bfloat16 [4, 16384, 4096], P('rep', 'fsdp'), may hold values from -6 to 6
- cotangent: bfloat16 [4, 16384, 1024], P('rep', 'fsdp'), may hold values from -0.046875 to 0.046875
- momentum: float32 [4, 4096, 1024], P('rep', 'fsdp'), may hold values from -6 to 6
Outputs:
- momentum_next: float32 [4, 4096, 1024], P('rep', 'fsdp')
- update: float32 [4096, 1024], P('fsdp')
All inputs are finite; a program needn't handle non-finite values.
Results may differ from a plain program's by a relative error of at most 0.0021.
Values sent between devices are 32-bit elements; how exact they have to be, the bound alone decides.
No kernel may reach another device: no remote copies, remote signals or barrier semaphores. Data moves between devices by JAX's collectives and lax.ppermute only.
A program may use at most 128 MiB of HBM per device.

v0:
```python
import jax
import jax.numpy as jnp
from jax import lax
from jax.sharding import PartitionSpec as P

CH = 64
BAND = 16
momentum_decay = 0.9


def basis_rows(size, keep):
    freq = jnp.arange(keep, dtype=jnp.float32)[:, None]
    point = jnp.arange(size, dtype=jnp.float32)[None, :]
    waves = jnp.cos(jnp.pi * (2.0 * point + 1.0) * freq / (2.0 * size))
    scales = jnp.where(freq == 0.0, jnp.sqrt(1.0 / size), jnp.sqrt(2.0 / size))
    return waves * scales


def bands_of(field, basis):
    rows, width = field.shape
    blocks = field.reshape(rows // CH, CH, width // CH, CH)
    return jnp.einsum("kn,anbm,lm->akbl", basis, blocks, basis, precision=lax.Precision.HIGHEST)


def term_maker(normed, part):
    return lax.dot_general(
        normed, part, (((0,), (0,)), ((), ())), preferred_element_type=jnp.float32
    )


def settle(grad, field, basis):
    accumulated = momentum_decay * field + grad
    bands = bands_of(accumulated, basis)
    count, _, wide, _ = bands.shape
    blocks = jnp.einsum("kn,akbl,lm->anbm", basis, bands, basis, precision=lax.Precision.HIGHEST)
    return (accumulated - blocks.reshape(count * CH, wide * CH), bands)


def body(activations, cotangent, momentum):
    values = activations[0].astype(jnp.float32)
    stat = jnp.mean(values * values, axis=-1, keepdims=True)
    normed = (values * lax.rsqrt(stat + 1e-05)).astype(jnp.bfloat16)
    targets = cotangent[0]
    field = momentum[0]
    basis = basis_rows(CH, BAND)
    grad = lax.psum_scatter(term_maker(normed, targets), "fsdp", scatter_dimension=0, tiled=True)
    cleared, bands = settle(grad, field, basis)
    count, _, wide, _ = bands.shape
    summed = lax.psum(bands, "rep")
    blocks = jnp.einsum("kn,akbl,lm->anbm", basis, summed, basis, precision=lax.Precision.HIGHEST)
    update = blocks.reshape(count * CH, wide * CH)
    groups = lax.axis_size("rep")
    return (cleared[None], update / groups)


def solution(mesh):
    return jax.shard_map(
        body,
        mesh=mesh,
        in_specs=(P("rep", "fsdp", None), P("rep", "fsdp", None), P("rep", "fsdp", None)),
        out_specs=(P("rep", "fsdp", None), P("fsdp", None)),
        check_vma=False,
    )
```

profile of v0, /device:TPU:0, one launch (start us, length us, event | category | flops | bytes accessed | tf_op | source)
XLA Modules:
  0.0 262.0 jit_solution(10249392141727543123)
XLA Ops:
  7.2 0.0 reduce-scatter.2.cloned.1.call-start
  7.2 0.0 copy-start
  7.2 7.6 %fusion = f32[2048]{0:T(1024)S(1)} fusion(bf16[1,2048,4096]{2,1,0:T(8,128)(2,1)} %param.3), kind=kLoop, calls=%fused_computation.2 | loop fusion | flops 25163776 | bytes 16785408 | tf_op jit(solution)/shard_map/reduce_sum | solution.py:41
  14.8 3.1 %copy-done = bf16[1,2048,4096]{2,1,0:T(8,128)(2,1)S(1)} copy-done((bf16[1,2048,4096]{2,1,0:T(8,128)(2,1)S(1)}, bf16[1,2048,4096]{2,1,0:T(8,128)(2,1)}, u32[]{:S(2)}) %copy-start) | copy-done | bytes 16777240
  17.9 23.4 %fusion.3 = f32[4096,1024]{1,0:T(8,128)} fusion(bf16[1,2048,4096]{2,1,0:T(8,128)(2,1)S(1)} %copy-done, f32[2048]{0:T(1024)S(1)} %add_rsqrt_fusion, bf16[1,2048,1024]{2,1,0:T(8,128)(2,1)} %param.4), kind=kOutput, calls=%fused_computation.5 | convolution fusion | flops 17205035008 | bytes 37756928 | tf_op jit(solution)/shard_map/dot_general | solution.py:26
  41.3 0.0 reduce-scatter.2.cloned.1.call-update
  41.3 119.0 %reduce-scatter.2.cloned.1.call-done = f32[512,1024]{1,0:T(8,128)} async-done(((f32[4096,1024]{1,0:T(8,128)}), f32[512,1024]{1,0:T(8,128)}) %reduce-scatter.2.cloned.1.call-update) | async-done | bytes 2097168 | tf_op jit(solution)/shard_map/reduce_scatter | solution.py:46
  160.3 2.7 %bitcast_add_fusion = f32[512,1024]{1,0:T(8,128)S(1)} fusion(f32[512,1024]{1,0:T(8,128)} %reduce-scatter.2.cloned.1.call-done, f32[1,512,1024]{2,1,0:T(8,128)} %param.5), kind=kLoop, calls=%fused_computation.12 | loop fusion | flops 1048576 | bytes 6291456 | tf_op jit(solution)/shard_map/add | solution.py:32
  163.0 2.5 reshape.49
  165.5 5.6 %fusion.7 = f32[8,16,64,16]{2,3,1,0:T(8,128)S(1)} fusion(f32[8,64,16,64]{3,2,1,0:T(8,128)} %reshape.49, f32[16]{0:T(128)S(1)} %compare_select_fusion, f32[64]{0:T(128)S(1)} %add_multiply_fusion), kind=kOutput, calls=%fused_computation.8 | convolution fusion | flops 100666368 | bytes 2621760 | tf_op jit(solution)/shard_map/kn,anbm,lm->akbl/dot_general | solution.py:22
  171.1 1.0 convolution_bitcast_fusion.1
  172.1 2.8 %fusion.13 = f32[8,16,16,64]{3,2,1,0:T(8,128)} fusion(f32[8,16,16,16]{3,1,2,0:T(8,128)S(1)} %convolution_bitcast_fusion.1, f32[16]{0:T(128)S(1)} %compare_select_fusion, f32[64]{0:T(128)S(1)} %add_multiply_fusion), kind=kOutput, calls=%fused_computation.19 | convolution fusion | flops 25168896 | bytes 655680 | tf_op jit(solution)/shard_map/kn,akbl,lm->anbm/dot_general | solution.py:35
  174.9 0.0 all-reduce.2.cloned.1.call-start
  174.9 9.3 %convolution_bitcast_fusion = f32[8,64,16,64]{3,1,2,0:T(8,128)} fusion(f32[8,16,16,64]{3,2,1,0:T(8,128)} %fusion.13, f32[16]{0:T(128)S(1)} %compare_select_fusion, f32[64]{0:T(128)S(1)} %add_multiply_fusion), kind=kOutput, calls=%fused_computation.11 | convolution fusion | flops 100666368 | bytes 2621760 | tf_op jit(solution)/shard_map/kn,akbl,lm->anbm/dot_general | solution.py:35
  184.2 0.0 copy-done.1
  184.2 0.0 all-reduce.2.cloned.1.call-update
  184.2 6.5 %copy.6 = f32[8,64,16,64]{3,2,1,0:T(8,128)} copy(f32[8,64,16,64]{3,1,2,0:T(8,128)} %convolution_bitcast_fusion) | data formatting | bytes 4194304 | tf_op jit(solution)/shard_map/kn,akbl,lm->anbm/transpose | solution.py:35
  190.8 4.8 %reshape.50 = f32[512,1024]{1,0:T(8,128)} reshape(f32[8,64,16,64]{3,2,1,0:T(8,128)} %copy.6) | data formatting | bytes 4194304 | tf_op jit(solution)/shard_map/reshape | solution.py:36
  195.6 3.3 %subtract_bitcast_fusion = f32[1,512,1024]{2,1,0:T(8,128)} fusion(f32[512,1024]{1,0:T(8,128)S(1)} %bitcast_add_fusion, f32[512,1024]{1,0:T(8,128)} %reshape.50), kind=kLoop, calls=%fused_computation.13 | loop fusion | flops 524288 | bytes 6291456 | tf_op jit(solution)/shard_map/broadcast_in_dim | solution.py:53
  198.9 37.4 %all-reduce.2.cloned.1.call-done = f32[8,16,16,16]{3,1,2,0:T(8,128)} async-done(((f32[8,16,16,16]{3,1,2,0:T(8,128)}), f32[8,16,16,16]{3,1,2,0:T(8,128)}) %all-reduce.2.cloned.1.call-update) | async-done | bytes 131088 | tf_op jit(solution)/shard_map/psum | solution.py:49
  236.3 3.0 %fusion.10 = f32[8,16,16,64]{3,2,1,0:T(8,128)S(1)} fusion(f32[8,16,16,16]{3,1,2,0:T(8,128)} %all-reduce.2.cloned.1.call-done, f32[16]{0:T(128)S(1)} %compare_select_fusion, f32[64]{0:T(128)S(1)} %add_multiply_fusion), kind=kOutput, calls=%fused_computation.16 | convolution fusion | flops 25168896 | bytes 655680 | tf_op jit(solution)/shard_map/kn,akbl,lm->anbm/dot_general | solution.py:50
  239.3 6.7 %multiply_bitcast_fusion = f32[8,64,16,64]{3,1,2,0:T(8,128)S(1)} fusion(f32[8,16,16,64]{3,2,1,0:T(8,128)S(1)} %fusion.10, f32[16]{0:T(128)S(1)} %compare_select_fusion, f32[64]{0:T(128)S(1)} %add_multiply_fusion), kind=kOutput, calls=%fused_computation.10 | convolution fusion | flops 101190656 | bytes 2621760 | tf_op jit(solution)/shard_map/kn,akbl,lm->anbm/dot_general | solution.py:50
  246.1 4.3 %copy.7 = f32[8,64,16,64]{3,2,1,0:T(8,128)} copy(f32[8,64,16,64]{3,1,2,0:T(8,128)S(1)} %multiply_bitcast_fusion) | data formatting | bytes 4194304 | tf_op jit(solution)/shard_map/div | solution.py:53
  250.4 4.8 %div.39 = f32[512,1024]{1,0:T(8,128)} reshape(f32[8,64,16,64]{3,2,1,0:T(8,128)} %copy.7) | data formatting | bytes 4194304 | tf_op jit(solution)/shard_map/div | solution.py:53
  (4 shorter events, 0.0 us)
Async XLA Ops:
  7.2 153.2 %reduce-scatter.2.cloned.1.call-start = ((), (), s32[]{:S(2)}) async-start(), calls=%async_computation.1 | async-start | bytes 18874368 | tf_op jit(solution)/shard_map/reduce_scatter | solution.py:46
  7.2 10.7 %copy-start = (bf16[1,2048,4096]{2,1,0:T(8,128)(2,1)S(1)}, bf16[1,2048,4096]{2,1,0:T(8,128)(2,1)}, u32[]{:S(2)}) copy-start(bf16[1,2048,4096]{2,1,0:T(8,128)(2,1)} %param.3) | copy-start | bytes 50331652
  172.1 12.1 %copy-start.1 = (f32[8,16,16,16]{3,1,2,0:T(8,128)}, f32[8,16,16,16]{3,1,2,0:T(8,128)S(1)}, u32[]{:S(2)}) copy-start(f32[8,16,16,16]{3,1,2,0:T(8,128)S(1)} %convolution_bitcast_fusion.1) | copy-start | bytes 393220
  174.9 61.4 %all-reduce.2.cloned.1.call-start = ((), (), s32[]{:S(2)}) async-start(), calls=%async_computation.2 | async-start | bytes 2097152 | tf_op jit(solution)/shard_map/psum | solution.py:49
Sparse Core Ops, SparseCore 0:
  41.4 118.8 reduce-scatter.1
  184.4 51.8 all-reduce.1
where the time goes:
time: 262 us
  waiting for transfers between devices  156 us (60%)
  matrix products  51.8 us (20%)
  local copies, waits for them, and re-layouts  26.1 us (10%)
  between operations  14.1 us (5%)
  other arithmetic  13.6 us (5%)
    reduce_scatter x1, waiting for transfers between devices, body(): lax.psum_scatter(term_maker(normed, targets), 'fsdp', scatter_dimension=0...  119 us
    psum x1, waiting for transfers between devices, body(): summed = lax.psum(bands, 'rep')  37.4 us
    dot_general x1, matrix products, term_maker(): lax.dot_general(normed, part, (((0,), (0,)), ((), ())), preferred_element...  23.4 us
    dot_general x2, matrix products, settle(): jnp.einsum('kn,akbl,lm->anbm', basis, bands, basis, precision=lax.Precisi...  12.1 us
    dot_general x2, matrix products, body(): jnp.einsum('kn,akbl,lm->anbm', basis, summed, basis, precision=lax.Precis...  9.76 us
    div x2, local copies, waits for them, and re-layouts, body(): return (cleared[None], update / groups)  9.14 us
    reduce_sum x1, other arithmetic, body(): stat = jnp.mean(values * values, axis=-1, keepdims=True)  7.6 us
    dot_general x2, matrix products, bands_of(): jnp.einsum('kn,anbm,lm->akbl', basis, blocks, basis, precision=lax.Precis...  6.6 us
  transfers between devices with their start and end apart: 2, of which 2 were waited for; matrix products, arithmetic and copies ran while one was open for 6% of the time, Pallas kernels for 0%

commit v1 on v0

--- a/solution.py
+++ b/solution.py
@@ -46,7 +46,7 @@
     grad = lax.psum_scatter(term_maker(normed, targets), "fsdp", scatter_dimension=0, tiled=True)
     cleared, bands = settle(grad, field, basis)
     count, _, wide, _ = bands.shape
-    summed = lax.psum(bands, "rep")
+    summed = jnp.sum(lax.all_gather(bands, "rep"), axis=0)
     blocks = jnp.einsum("kn,akbl,lm->anbm", basis, summed, basis, precision=lax.Precision.HIGHEST)
     update = blocks.reshape(count * CH, wide * CH)
     groups = lax.axis_size("rep")

time: 262 us -> 293 us (1.12)
  blocking collectives: 0 us -> 71.6 us
  waiting for transfers between devices: 156 us -> 119 us
  matrix products: 51.8 us -> 47.3 us
    all_gather x0 -> x1, blocking collectives: none -> 71.6 us  [body(): summed = jnp.sum(lax.all_gather(bands, 'rep'), axis=0)]
    psum x1 -> x0, waiting for transfers between devices: 37.4 us -> none  [body(): summed = lax.psum(bands, 'rep')]
    dot_general x2, matrix products: 12.1 us -> 8.54 us  [settle(): jnp.einsum('kn,akbl,lm->anbm', basis, bands, basis, precision=lax.Precisi...]
  transfers between devices with their start and end apart: 2 -> 1, of which waited for: 2 -> 1; matrix products, arithmetic and copies ran while one was open for 6% -> 0% of each run, Pallas kernels for 0% -> 0%
where the time goes in v1:
time: 293 us
  waiting for transfers between devices  119 us (41%)
  blocking collectives  71.6 us (24%)
  matrix products  47.3 us (16%)
  local copies, waits for them, and re-layouts  24.2 us (8%)
  other arithmetic  16.3 us (6%)
  between operations  14.1 us (5%)
    reduce_scatter x1, waiting for transfers between devices, body(): lax.psum_scatter(term_maker(normed, targets), 'fsdp', scatter_dimension=0...  119 us
    all_gather x1, blocking collectives, body(): summed = jnp.sum(lax.all_gather(bands, 'rep'), axis=0)  71.6 us
    dot_general x1, matrix products, term_maker(): lax.dot_general(normed, part, (((0,), (0,)), ((), ())), preferred_element...  23.4 us
    div x2, local copies, waits for them, and re-layouts, body(): return (cleared[None], update / groups)  9.14 us
    dot_general x2, matrix products, body(): jnp.einsum('kn,akbl,lm->anbm', basis, summed, basis, precision=lax.Precis...  8.65 us
    dot_general x2, matrix products, settle(): jnp.einsum('kn,akbl,lm->anbm', basis, bands, basis, precision=lax.Precisi...  8.54 us
    reduce_sum x1, other arithmetic, body(): stat = jnp.mean(values * values, axis=-1, keepdims=True)  7.6 us
    dot_general x2, matrix products, bands_of(): jnp.einsum('kn,anbm,lm->akbl', basis, blocks, basis, precision=lax.Precis...  6.78 us
  transfers between devices with their start and end apart: 1, of which 1 were waited for; matrix products, arithmetic and copies ran while one was open for 0% of the time, Pallas kernels for 0%

profile of v1, /device:TPU:0, one launch (start us, length us, event | category | flops | bytes accessed | tf_op | source)
XLA Modules:
  0.0 292.6 jit_solution(11358705074118501277)
XLA Ops:
  7.2 0.0 reduce-scatter.2.cloned.1.call-start
  7.2 0.0 copy-start
  7.2 7.6 %fusion = f32[2048]{0:T(1024)S(1)} fusion(bf16[1,2048,4096]{2,1,0:T(8,128)(2,1)} %param.3), kind=kLoop, calls=%fused_computation.2 | loop fusion | flops 25163776 | bytes 16785408 | tf_op jit(solution)/shard_map/reduce_sum | solution.py:41
  14.8 3.1 %copy-done = bf16[1,2048,4096]{2,1,0:T(8,128)(2,1)S(1)} copy-done((bf16[1,2048,4096]{2,1,0:T(8,128)(2,1)S(1)}, bf16[1,2048,4096]{2,1,0:T(8,128)(2,1)}, u32[]{:S(2)}) %copy-start) | copy-done | bytes 16777240
  17.9 23.4 %fusion.3 = f32[4096,1024]{1,0:T(8,128)} fusion(bf16[1,2048,4096]{2,1,0:T(8,128)(2,1)S(1)} %copy-done, f32[2048]{0:T(1024)S(1)} %add_rsqrt_fusion, bf16[1,2048,1024]{2,1,0:T(8,128)(2,1)} %param.4), kind=kOutput, calls=%fused_computation.5 | convolution fusion | flops 17205035008 | bytes 37756928 | tf_op jit(solution)/shard_map/dot_general | solution.py:26
  41.3 0.0 reduce-scatter.2.cloned.1.call-update
  41.3 119.0 %reduce-scatter.2.cloned.1.call-done = f32[512,1024]{1,0:T(8,128)} async-done(((f32[4096,1024]{1,0:T(8,128)}), f32[512,1024]{1,0:T(8,128)}) %reduce-scatter.2.cloned.1.call-update) | async-done | bytes 2097168 | tf_op jit(solution)/shard_map/reduce_scatter | solution.py:46
  160.3 2.7 bitcast_add_fusion
  163.0 2.5 reshape.49
  165.5 5.8 %fusion.7 = f32[8,16,64,16]{2,3,1,0:T(8,128)S(1)} fusion(f32[8,64,16,64]{3,2,1,0:T(8,128)} %reshape.49, f32[16]{0:T(128)S(1)} %compare_select_fusion, f32[64]{0:T(128)S(1)} %add_multiply_fusion), kind=kOutput, calls=%fused_computation.8 | convolution fusion | flops 100666368 | bytes 2621760 | tf_op jit(solution)/shard_map/kn,anbm,lm->akbl/dot_general | solution.py:22
  171.3 1.0 convolution_bitcast_fusion.1
  172.3 1.8 fusion.14
  174.1 0.3 copy.11
  174.4 6.7 %convolution_bitcast_fusion = f32[8,64,16,64]{3,1,2,0:T(8,128)S(1)} fusion(f32[8,16,16,64]{3,2,1,0:T(8,128)S(1)} %fusion.14, f32[16]{0:T(128)S(1)} %compare_select_fusion, f32[64]{0:T(128)S(1)} %add_multiply_fusion), kind=kOutput, calls=%fused_computation.11 | convolution fusion | flops 100666368 | bytes 2621760 | tf_op jit(solution)/shard_map/kn,akbl,lm->anbm/dot_general | solution.py:35
  181.2 4.3 %copy.10 = f32[8,64,16,64]{3,2,1,0:T(8,128)} copy(f32[8,64,16,64]{3,1,2,0:T(8,128)S(1)} %convolution_bitcast_fusion) | data formatting | bytes 4194304 | tf_op jit(solution)/shard_map/kn,akbl,lm->anbm/transpose | solution.py:35
  185.5 4.8 %reshape.50 = f32[512,1024]{1,0:T(8,128)} reshape(f32[8,64,16,64]{3,2,1,0:T(8,128)} %copy.10) | data formatting | bytes 4194304 | tf_op jit(solution)/shard_map/reshape | solution.py:36
  190.3 3.3 %subtract_bitcast_fusion = f32[1,512,1024]{2,1,0:T(8,128)} fusion(f32[512,1024]{1,0:T(8,128)S(1)} %bitcast_add_fusion, f32[512,1024]{1,0:T(8,128)} %reshape.50), kind=kLoop, calls=%fused_computation.13 | loop fusion | flops 524288 | bytes 6291456 | tf_op jit(solution)/shard_map/broadcast_in_dim | solution.py:53
  193.6 71.6 %all-gather = f32[32,16,16,16]{3,2,1,0:T(8,128)} all-gather(f32[8,16,16,16]{3,2,1,0:T(8,128)S(1)} %copy.11), channel_id=2, replica_groups=mesh['rep'=4,'fsdp'=8] {'rep'}, dimensions={0}, use_global_device_ids=true | all-gather | bytes 655360 | tf_op jit(solution)/shard_map/all_gather | solution.py:49
  265.2 2.7 reduce_sum.19
  267.9 1.9 fusion.9
  269.8 6.7 %multiply_bitcast_fusion = f32[8,64,16,64]{3,1,2,0:T(8,128)S(1)} fusion(f32[8,16,16,64]{3,2,1,0:T(8,128)S(1)} %fusion.9, f32[16]{0:T(128)S(1)} %compare_select_fusion, f32[64]{0:T(128)S(1)} %add_multiply_fusion), kind=kOutput, calls=%fused_computation.10 | convolution fusion | flops 101190656 | bytes 2621760 | tf_op jit(solution)/shard_map/kn,akbl,lm->anbm/dot_general | solution.py:50
  276.6 4.3 %copy.14 = f32[8,64,16,64]{3,2,1,0:T(8,128)} copy(f32[8,64,16,64]{3,1,2,0:T(8,128)S(1)} %multiply_bitcast_fusion) | data formatting | bytes 4194304 | tf_op jit(solution)/shard_map/div | solution.py:53
  280.9 4.8 %div.39 = f32[512,1024]{1,0:T(8,128)} reshape(f32[8,64,16,64]{3,2,1,0:T(8,128)} %copy.14) | data formatting | bytes 4194304 | tf_op jit(solution)/shard_map/div | solution.py:53
  (3 shorter events, 0.0 us)
Async XLA Ops:
  7.2 153.2 %reduce-scatter.2.cloned.1.call-start = ((), (), s32[]{:S(2)}) async-start(), calls=%async_computation.1 | async-start | bytes 18874368 | tf_op jit(solution)/shard_map/reduce_scatter | solution.py:46
  7.2 10.7 %copy-start = (bf16[1,2048,4096]{2,1,0:T(8,128)(2,1)S(1)}, bf16[1,2048,4096]{2,1,0:T(8,128)(2,1)}, u32[]{:S(2)}) copy-start(bf16[1,2048,4096]{2,1,0:T(8,128)(2,1)} %param.3) | copy-start | bytes 50331652
Sparse Core Ops, SparseCore 0:
  41.4 118.8 reduce-scatter.1
